TPU v7x, 32 devices: a whole 2x2x4 slice. The times are simulated.
32 devices in a mesh: dp: 8 (over z, x), mp: 4 (over y, core).
Axes of the slice: x: 2, y: 2, z: 4, core: 2. Of those that a mesh axis runs over, the one named last changes fastest.
Arguments:
- text_blocks: bfloat16 [256, 64, 768], P(('dp', 'mp')), may hold values from -6 to 6
- visual_blocks: bfloat16 [256, 40, 768], P(('dp', 'mp')), may hold values from -6 to 6
- drop_flags: int32 [256, 2], P('dp'), may hold values 0 or 1
- qkv_weight: bfloat16 [4, 768, 3, 768], P(None, None, None, 'mp'), may hold values from -0.21875 to 0.21875
- out_weight: bfloat16 [4, 768, 768], P(None, 'mp'), may hold values from -0.625 to 0.625
- up_weight: bfloat16 [2, 768, 3072], P(None, None, 'mp'), may hold values from -0.21875 to 0.21875
- down_weight: bfloat16 [2, 3072, 768], P(None, 'mp'), may hold values from -0.109375 to 0.109375
- norm_gain: float32 [6, 768], replicated, may hold values from 0.5 to 1.5
- norm_shift: float32 [6, 768], replicated, may hold values from -3 to 3
- text_cotangent: bfloat16 [256, 64, 768], P(('dp', 'mp')), may hold values from -6 to 6
- visual_cotangent: bfloat16 [256, 40, 768], P(('dp', 'mp')), may hold values from -6 to 6
Outputs:
- text_output: bfloat16 [256, 64, 768], P(('dp', 'mp'))
- visual_output: bfloat16 [256, 40, 768], P(('dp', 'mp'))
- text_gradient: bfloat16 [256, 64, 768], P(('dp', 'mp'))
- visual_gradient: bfloat16 [256, 40, 768], P(('dp', 'mp'))
- qkv_gradient: float32 [4, 768, 3, 768], P(None, None, None, 'mp')
- out_gradient: float32 [4, 768, 768], P(None, 'mp')
- up_gradient: float32 [2, 768, 3072], P(None, None, 'mp')
- down_gradient: float32 [2, 3072, 768], P(None, 'mp')
- gain_gradient: float32 [6, 768], replicated
- shift_gradient: float32 [6, 768], replicated
Inputs may be any that keep to these rules, and one draw needn't show every extreme that they name: drop_flags[:, 0] = 1 marks a page whose text is absent, drop_flags[:, 1] = 1 one whose visual blocks are absent.
All inputs are finite; a program needn't handle non-finite values.
Results may differ from a plain program's by a relative error of at most 0.025.
Values may be sent and summed in bfloat16 or wider, within the bound.
No kernel may reach another device: no remote copies, remote signals or barrier semaphores. Data moves between devices by JAX's collectives and lax.ppermute only.
A program may use at most 256 MiB of HBM per device.

v0:
```python
import jax
import jax.numpy as jnp
from jax import lax
from jax.sharding import PartitionSpec as P

HEAD = 64
EPSILON = 1e-05


def normalize(values, gain, shift):
    center = values - jnp.mean(values, axis=-1, keepdims=True)
    spread = jnp.mean(center * center, axis=-1, keepdims=True)
    return center * lax.rsqrt(spread + EPSILON) * gain + shift


def linear(activation, weight):
    return jnp.einsum("pld,de->ple", activation, weight, preferred_element_type=jnp.float32)


def linear_back(gradient, weight):
    return jnp.einsum("ple,de->pld", gradient, weight, preferred_element_type=jnp.float32)


def weight_grad(activation, gradient):
    return jnp.einsum("pld,ple->de", activation, gradient, preferred_element_type=jnp.float32)


def split_heads(values):
    return values.reshape(values.shape[0], values.shape[1], values.shape[2] // HEAD, HEAD)


def merge_heads(values):
    return values.reshape(values.shape[0], values.shape[1], values.shape[2] * values.shape[3])


def score_block(queries, key_block):
    raw = jnp.einsum(
        "pqhe,pkhe->phqk",
        split_heads(queries),
        split_heads(key_block),
        preferred_element_type=jnp.float32,
    )
    return raw * HEAD ** (-0.5)


def attend_context(query_side, key_side, weight_block, keep_mask):
    queries = linear(query_side, weight_block[:, 0]).astype(jnp.bfloat16)
    key_block = linear(key_side, weight_block[:, 1]).astype(jnp.bfloat16)
    value_block = linear(key_side, weight_block[:, 2]).astype(jnp.bfloat16)
    scores = score_block(queries, key_block)
    row_max = jnp.max(scores, axis=-1, keepdims=True)
    log_total = row_max + jnp.log(jnp.sum(jnp.exp(scores - row_max), axis=-1, keepdims=True))
    probability = jnp.exp(scores - log_total).astype(jnp.bfloat16)
    context = merge_heads(
        jnp.einsum(
            "phqk,pkhe->pqhe",
            probability,
            split_heads(value_block),
            preferred_element_type=jnp.float32,
        )
    )
    if keep_mask is not None:
        context = context * keep_mask[:, None, None]
    context = context.astype(jnp.bfloat16)
    return (context, (queries, key_block, value_block, log_total, context))


def attend_back(query_side, key_side, weight_block, out_block, keep_mask, saved, out_grad):
    queries, key_block, value_block, log_total, context = saved
    out_weight_grad = weight_grad(context, out_grad)
    context_grad = linear_back(out_grad, out_block).astype(jnp.bfloat16)
    if keep_mask is not None:
        context_grad = context_grad * keep_mask[:, None, None].astype(jnp.bfloat16)
    probability = jnp.exp(score_block(queries, key_block) - log_total)
    heads_grad = split_heads(context_grad)
    prob_grad = jnp.einsum(
        "pqhe,pkhe->phqk", heads_grad, split_heads(value_block), preferred_element_type=jnp.float32
    )
    value_grad = merge_heads(
        jnp.einsum(
            "phqk,pqhe->pkhe",
            probability.astype(jnp.bfloat16),
            heads_grad,
            preferred_element_type=jnp.float32,
        )
    ).astype(jnp.bfloat16)
    score_grad = (
        probability * (prob_grad - jnp.sum(prob_grad * probability, axis=-1, keepdims=True))
    ).astype(jnp.bfloat16)
    query_grad = (
        merge_heads(
            jnp.einsum(
                "phqk,pkhe->pqhe",
                score_grad,
                split_heads(key_block),
                preferred_element_type=jnp.float32,
            )
        )
        * HEAD ** (-0.5)
    ).astype(jnp.bfloat16)
    key_grad = (
        merge_heads(
            jnp.einsum(
                "phqk,pqhe->pkhe",
                score_grad,
                split_heads(queries),
                preferred_element_type=jnp.float32,
            )
        )
        * HEAD ** (-0.5)
    ).astype(jnp.bfloat16)
    in_weight_grad = jnp.stack(
        [
            weight_grad(query_side, query_grad),
            weight_grad(key_side, key_grad),
            weight_grad(key_side, value_grad),
        ],
        axis=1,
    )
    query_back = linear_back(query_grad, weight_block[:, 0])
    key_back = linear_back(key_grad, weight_block[:, 1]) + linear_back(
        value_grad, weight_block[:, 2]
    )
    return (in_weight_grad, out_weight_grad, query_back, key_back)


def feed_forward(activation, up_block, down_block):
    before = linear(activation, up_block)
    hidden = jax.nn.gelu(before).astype(jnp.bfloat16)
    return (linear(hidden, down_block), (before, hidden))


def feed_back(activation, up_block, down_block, saved, out_grad):
    before, hidden = saved
    down_grad = weight_grad(hidden, out_grad)
    hidden_grad = linear_back(out_grad, down_block)
    gelu_pull = jax.vjp(jax.nn.gelu, before)[1]
    before_grad = gelu_pull(hidden_grad)[0].astype(jnp.bfloat16)
    up_grad = weight_grad(activation, before_grad)
    return (up_grad, down_grad, linear_back(before_grad, up_block))


def per_device(
    text_blocks,
    visual_blocks,
    drop_flags,
    qkv_weight,
    out_weight,
    up_weight,
    down_weight,
    norm_gain,
    norm_shift,
    text_cotangent,
    visual_cotangent,
):
    keep_text = (1 - drop_flags[:, 0]).astype(jnp.float32)
    keep_visual = (1 - drop_flags[:, 1]).astype(jnp.float32)
    text_now = text_blocks.astype(jnp.float32)
    visual_now = visual_blocks.astype(jnp.float32)
    inputs = []
    gathered = []
    saved = []
    for sublayer in range(3):
        inputs.append((text_now, visual_now))
        text_norm = normalize(text_now, norm_gain[2 * sublayer], norm_shift[2 * sublayer]).astype(
            jnp.bfloat16
        )
        visual_norm = normalize(
            visual_now, norm_gain[2 * sublayer + 1], norm_shift[2 * sublayer + 1]
        ).astype(jnp.bfloat16)
        text_rows, visual_rows = (
            lax.all_gather(text_norm, "mp", axis=0, tiled=True),
            lax.all_gather(visual_norm, "mp", axis=0, tiled=True),
        )
        gathered.append((text_rows, visual_rows))
        text_part = None
        visual_part = None
        if sublayer < 2:
            if sublayer == 0:
                text_context, text_saved = attend_context(
                    text_rows, visual_rows, qkv_weight[0], keep_visual
                )
                visual_context, visual_saved = attend_context(
                    visual_rows, text_rows, qkv_weight[1], keep_text
                )
            else:
                text_context, text_saved = attend_context(text_rows, text_rows, qkv_weight[2], None)
                visual_context, visual_saved = attend_context(
                    visual_rows, visual_rows, qkv_weight[3], None
                )
            text_part = linear(text_context, out_weight[2 * sublayer])
            visual_part = linear(visual_context, out_weight[2 * sublayer + 1])
        else:
            text_part, text_saved = feed_forward(text_rows, up_weight[0], down_weight[0])
            visual_part, visual_saved = feed_forward(visual_rows, up_weight[1], down_weight[1])
        text_added, visual_added = (
            lax.psum_scatter(
                text_part.astype(jnp.bfloat16), "mp", scatter_dimension=0, tiled=True
            ).astype(jnp.float32),
            lax.psum_scatter(
                visual_part.astype(jnp.bfloat16), "mp", scatter_dimension=0, tiled=True
            ).astype(jnp.float32),
        )
        saved.append((text_saved, visual_saved))
        text_now = text_now + text_added
        visual_now = visual_now + visual_added
    text_output = text_now.astype(jnp.bfloat16)
    visual_output = visual_now.astype(jnp.bfloat16)
    text_back = text_cotangent.astype(jnp.float32)
    visual_back = visual_cotangent.astype(jnp.float32)
    in_parts = [None, None, None, None]
    out_parts = [None, None, None, None]
    gain_parts = [None, None, None, None, None, None]
    shift_parts = [None, None, None, None, None, None]
    up_grads = None
    down_grads = None
    for sublayer in (2, 1, 0):
        text_branch, visual_branch = (
            lax.all_gather(text_back.astype(jnp.bfloat16), "mp", axis=0, tiled=True),
            lax.all_gather(visual_back.astype(jnp.bfloat16), "mp", axis=0, tiled=True),
        )
        text_rows, visual_rows = gathered[sublayer]
        text_saved, visual_saved = saved[sublayer]
        if sublayer == 2:
            up_text, down_text, text_part = feed_back(
                text_rows, up_weight[0], down_weight[0], text_saved, text_branch
            )
            up_visual, down_visual, visual_part = feed_back(
                visual_rows, up_weight[1], down_weight[1], visual_saved, visual_branch
            )
            up_grads = jnp.stack([up_text, up_visual])
            down_grads = jnp.stack([down_text, down_visual])
        elif sublayer == 1:
            in_parts[2], out_parts[2], query_back, key_back = attend_back(
                text_rows, text_rows, qkv_weight[2], out_weight[2], None, text_saved, text_branch
            )
            text_part = query_back + key_back
            in_parts[3], out_parts[3], query_back, key_back = attend_back(
                visual_rows,
                visual_rows,
                qkv_weight[3],
                out_weight[3],
                None,
                visual_saved,
                visual_branch,
            )
            visual_part = query_back + key_back
        else:
            in_parts[0], out_parts[0], text_query_back, visual_key_back = attend_back(
                text_rows,
                visual_rows,
                qkv_weight[0],
                out_weight[0],
                keep_visual,
                text_saved,
                text_branch,
            )
            in_parts[1], out_parts[1], visual_query_back, text_key_back = attend_back(
                visual_rows,
                text_rows,
                qkv_weight[1],
                out_weight[1],
                keep_text,
                visual_saved,
                visual_branch,
            )
            text_part = text_query_back + text_key_back
            visual_part = visual_query_back + visual_key_back
        text_norm_grad, visual_norm_grad = (
            lax.psum_scatter(
                text_part.astype(jnp.bfloat16), "mp", scatter_dimension=0, tiled=True
            ).astype(jnp.float32),
            lax.psum_scatter(
                visual_part.astype(jnp.bfloat16), "mp", scatter_dimension=0, tiled=True
            ).astype(jnp.float32),
        )
        text_in, visual_in = inputs[sublayer]
        text_pull = jax.vjp(normalize, text_in, norm_gain[2 * sublayer], norm_shift[2 * sublayer])[
            1
        ]
        text_delta, gain_parts[2 * sublayer], shift_parts[2 * sublayer] = text_pull(text_norm_grad)
        visual_pull = jax.vjp(
            normalize, visual_in, norm_gain[2 * sublayer + 1], norm_shift[2 * sublayer + 1]
        )[1]
        visual_delta, gain_parts[2 * sublayer + 1], shift_parts[2 * sublayer + 1] = visual_pull(
            visual_norm_grad
        )
        text_back = text_back + text_delta
        visual_back = visual_back + visual_delta
    gain_grads = jnp.stack(gain_parts)
    shift_grads = jnp.stack(shift_parts)
    gain_grads, shift_grads = (
        lax.psum(gain_grads.astype(jnp.bfloat16), "mp").astype(jnp.float32),
        lax.psum(shift_grads.astype(jnp.bfloat16), "mp").astype(jnp.float32),
    )
    in_grads = jnp.stack(in_parts)
    out_grads = jnp.stack(out_parts)
    in_grads, out_grads, up_grads, down_grads = jax.tree.map(
        lambda grad: lax.psum(grad.astype(jnp.bfloat16), "dp").astype(jnp.float32),
        (in_grads, out_grads, up_grads, down_grads),
    )
    gain_grads, shift_grads = lax.psum((gain_grads, shift_grads), "dp")
    return (
        text_output,
        visual_output,
        text_back.astype(jnp.bfloat16),
        visual_back.astype(jnp.bfloat16),
        in_grads,
        out_grads,
        up_grads,
        down_grads,
        gain_grads,
        shift_grads,
    )


def solution(mesh):
    placed = (
        P(("dp", "mp"), None, None),
        P(("dp", "mp"), None, None),
        P("dp", None),
        P(None, None, None, "mp"),
        P(None, "mp", None),
        P(None, None, "mp"),
        P(None, "mp", None),
        P(),
        P(),
        P(("dp", "mp"), None, None),
        P(("dp", "mp"), None, None),
    )
    return jax.shard_map(
        per_device,
        mesh=mesh,
        in_specs=placed,
        out_specs=(
            P(("dp", "mp"), None, None),
            P(("dp", "mp"), None, None),
            P(("dp", "mp"), None, None),
            P(("dp", "mp"), None, None),
            P(None, None, None, "mp"),
            P(None, "mp", None),
            P(None, None, "mp"),
            P(None, "mp", None),
            P(),
            P(),
        ),
        check_vma=False,
    )
```

profile of v0, /device:TPU:0, one launch (start us, length us, event | category | flops | bytes accessed | tf_op | source)
XLA Modules:
  0.0 1164.1 jit_solution(13793235685979987641)
XLA Ops:
  20.7 18.6 %all-gather.13.cloned.1.call-done = bf16[32,40,768]{2,1,0:T(8,128)(2,1)} async-done(((bf16[8,40,768]{2,1,0:T(8,128)(2,1)}), bf16[32,40,768]{2,1,0:T(8,128)(2,1)}) %all-gather.13.cloned.1.call-update) | async-done | bytes 1966096 | tf_op jit(solution)/shard_map/all_gather | solution.py:173
  42.8 27.1 %all-gather.15.cloned.1.call-done = bf16[32,64,768]{2,1,0:T(8,128)(2,1)} async-done(((bf16[8,64,768]{2,1,0:T(8,128)(2,1)}), bf16[32,64,768]{2,1,0:T(8,128)(2,1)}) %all-gather.15.cloned.1.call-update) | async-done | bytes 3145744 | tf_op jit(solution)/shard_map/all_gather | solution.py:172
  69.9 3.9 convolution_convert_fusion.13
  75.6 4.4 convolution_convert_fusion.14
  100.8 4.1 convolution_convert_fusion.18
  114.1 3.9 convolution_convert_fusion.3
  118.0 5.9 reduce-scatter.19.cloned.1.call-done
  127.7 37.1 %reduce-scatter.13.cloned.1.call-done = bf16[8,64,768]{2,1,0:T(8,128)(2,1)} async-done(((bf16[32,64,768]{2,1,0:T(8,128)(2,1)}), bf16[8,64,768]{2,1,0:T(8,128)(2,1)}) %reduce-scatter.13.cloned.1.call-update) | async-done | bytes 786448 | tf_op jit(solution)/shard_map/reduce_scatter | solution.py:197
  168.6 20.0 %all-gather.21.cloned.1.call-done = bf16[32,40,768]{2,1,0:T(8,128)(2,1)} async-done(((bf16[8,40,768]{2,1,0:T(8,128)(2,1)}), bf16[32,40,768]{2,1,0:T(8,128)(2,1)}) %all-gather.21.cloned.1.call-update) | async-done | bytes 1966096 | tf_op jit(solution)/shard_map/all_gather | solution.py:173
  198.0 3.9 convolution_convert_fusion.26
  244.0 3.9 convolution_convert_fusion.2
  248.0 4.7 reduce-scatter.21.cloned.1.call-done
  256.6 37.1 %reduce-scatter.15.cloned.1.call-done = bf16[8,64,768]{2,1,0:T(8,128)(2,1)} async-done(((bf16[32,64,768]{2,1,0:T(8,128)(2,1)}), bf16[8,64,768]{2,1,0:T(8,128)(2,1)}) %reduce-scatter.15.cloned.1.call-update) | async-done | bytes 786448 | tf_op jit(solution)/shard_map/reduce_scatter | solution.py:197
  297.9 19.9 %all-gather.23.cloned.1.call-done = bf16[32,40,768]{2,1,0:T(8,128)(2,1)} async-done(((bf16[8,40,768]{2,1,0:T(8,128)(2,1)}), bf16[32,40,768]{2,1,0:T(8,128)(2,1)}) %all-gather.23.cloned.1.call-update) | async-done | bytes 1966096 | tf_op jit(solution)/shard_map/all_gather | solution.py:173
  317.7 5.5 fusion.80
  323.2 17.8 %all-gather.31.cloned.1.call-done = bf16[32,40,768]{2,1,0:T(8,128)(2,1)} async-done(((bf16[8,40,768]{2,1,0:T(8,128)(2,1)}), bf16[32,40,768]{2,1,0:T(8,128)(2,1)}) %all-gather.31.cloned.1.call-update) | async-done | bytes 1966096 | tf_op jit(solution)/shard_map/all_gather | solution.py:220
  341.0 7.0 fusion.13
  352.7 18.9 %all-gather.19.cloned.1.call-done = bf16[32,64,768]{2,1,0:T(8,128)(2,1)} async-done(((bf16[8,64,768]{2,1,0:T(8,128)(2,1)}), bf16[32,64,768]{2,1,0:T(8,128)(2,1)}) %all-gather.19.cloned.1.call-update) | async-done | bytes 3145744 | tf_op jit(solution)/shard_map/all_gather | solution.py:172
  371.7 7.5 fusion.85
  379.2 22.4 %all-gather.25.cloned.1.call-done = bf16[32,64,768]{2,1,0:T(8,128)(2,1)} async-done(((bf16[8,64,768]{2,1,0:T(8,128)(2,1)}), bf16[32,64,768]{2,1,0:T(8,128)(2,1)}) %all-gather.25.cloned.1.call-update) | async-done | bytes 3145744 | tf_op jit(solution)/shard_map/all_gather | solution.py:219
  401.7 8.5 fusion.6
  411.8 4.1 convolution_convert_fusion
  415.9 18.7 %reduce-scatter.29.cloned.1.call-done = bf16[8,40,768]{2,1,0:T(8,128)(2,1)} async-done(((bf16[32,40,768]{2,1,0:T(8,128)(2,1)}), bf16[8,40,768]{2,1,0:T(8,128)(2,1)}) %reduce-scatter.29.cloned.1.call-update) | async-done | bytes 491536 | tf_op jit(solution)/shard_map/reduce_scatter | solution.py:273
  439.9 35.0 %reduce-scatter.25.cloned.1.call-done = bf16[8,64,768]{2,1,0:T(8,128)(2,1)} async-done(((bf16[32,64,768]{2,1,0:T(8,128)(2,1)}), bf16[8,64,768]{2,1,0:T(8,128)(2,1)}) %reduce-scatter.25.cloned.1.call-update) | async-done | bytes 786448 | tf_op jit(solution)/shard_map/reduce_scatter | solution.py:270
  479.8 18.9 %all-gather.33.cloned.1.call-done = bf16[32,40,768]{2,1,0:T(8,128)(2,1)} async-done(((bf16[8,40,768]{2,1,0:T(8,128)(2,1)}), bf16[32,40,768]{2,1,0:T(8,128)(2,1)}) %all-gather.33.cloned.1.call-update) | async-done | bytes 1966096 | tf_op jit(solution)/shard_map/all_gather | solution.py:220
  537.0 6.3 convolution_convert_fusion.5
  543.6 4.3 convolution_convert_fusion.12
  550.5 4.2 multiply_reduce_fusion
  561.6 4.0 fusion.36
  578.4 8.7 convolution_convert_fusion.1
  590.3 10.0 reduce-scatter.23.cloned.1.call-done
  600.3 3.9 fusion.209
  608.0 4.5 reshape.443
  616.1 24.6 %reduce-scatter.27.cloned.1.call-done = bf16[8,64,768]{2,1,0:T(8,128)(2,1)} async-done(((bf16[32,64,768]{2,1,0:T(8,128)(2,1)}), bf16[8,64,768]{2,1,0:T(8,128)(2,1)}) %reduce-scatter.27.cloned.1.call-update) | async-done | bytes 786448 | tf_op jit(solution)/shard_map/reduce_scatter | solution.py:270
  643.9 37.2 %reduce-scatter.17.cloned.1.call-done = bf16[8,64,768]{2,1,0:T(8,128)(2,1)} async-done(((bf16[32,64,768]{2,1,0:T(8,128)(2,1)}), bf16[8,64,768]{2,1,0:T(8,128)(2,1)}) %reduce-scatter.17.cloned.1.call-update) | async-done | bytes 786448 | tf_op jit(solution)/shard_map/reduce_scatter | solution.py:197
  681.0 4.1 fusion.210
  685.4 5.1 fusion.44
  699.5 5.5 all-gather.35.cloned.1.call-done
  726.7 9.0 all-gather.29.cloned.1.call-done
  735.7 3.9 fusion.49
  769.6 8.5 fusion.45
  782.5 3.9 convolution_convert_fusion.8
  786.4 5.1 fusion.172
  799.2 4.1 add_convert_fusion
  803.6 5.7 fusion.43
  849.5 10.7 all-reduce.2
  860.2 40.7 %all-reduce = (f32[6,768]{1,0:T(8,128)}, f32[6,768]{1,0:T(8,128)}) all-reduce(bf16[6,768]{1,0:T(8,128)(2,1)S(1)} %get-tuple-element.40, bf16[6,768]{1,0:T(8,128)(2,1)S(1)} %get-tuple-element.41), channel_id=1, replica_groups=mesh['dp'=8,'mp'=4] {'dp'}, use_global_device_ids=true, to_apply=%region_59.0 | all-reduce | flops 9216 | bytes 55296 | tf_op jit(solution)/shard_map/psum | solution.py:302
  903.9 241.7 %all-reduce.5.cloned.1.call-done = (bf16[4,768,3,192]{1,3,2,0:T(8,128)(2,1)}, bf16[4,192,768]{2,1,0:T(8,128)(2,1)}, bf16[2,768,768]{2,1,0:T(8,128)(2,1)}, bf16[2,768,768]{2,1,0:T(8,128)(2,1)}) async-done(((bf16[4,768,3,192]{1,3,2,0:T(8,128)(2,1)}, bf16[4,192,768]{2,1,0:T(8,128)(2,1)}, bf16[2,768,768]{2,1,0:T(8,128)(2,1)}, bf16[2,768,768]{2,1,0:T(8,128)(2,1)}), (bf16[4,768,3,192]{1,3,2,0:T(8,128)(2,1)}, ...) | async-done | bytes 9437200 | tf_op jit(solution)/shard_map/psum | solution.py:299
  (524 shorter events, 333.7 us)
Async XLA Ops:
  7.2 7.4 copy-start
  7.2 32.1 %all-gather.13.cloned.1.call-start = ((), (), s32[]{:S(2)}) async-start(), calls=%async_computation.12 | async-start | bytes 2457600 | tf_op jit(solution)/shard_map/all_gather | solution.py:173
  8.5 6.1 copy-start.95
  14.5 55.4 %all-gather.15.cloned.1.call-start = ((), (), s32[]{:S(2)}) async-start(), calls=%async_computation.13 | async-start | bytes 3932160 | tf_op jit(solution)/shard_map/all_gather | solution.py:172
  14.8 5.8 copy-start.93
  15.2 5.5 copy-start.107
  16.5 107.4 %reduce-scatter.19.cloned.1.call-start = ((), (), s32[]{:S(2)}) async-start(), calls=%async_computation.19 | async-start | bytes 2457600 | tf_op jit(solution)/shard_map/reduce_scatter | solution.py:200
  17.1 68.9 %copy-start.111 = (f32[32]{0:T(128)}, f32[32]{0:T(128)S(1)}, u32[]{:S(2)}) copy-start(f32[32]{0:T(128)S(1)} %get-tuple-element.58) | copy-start | bytes 388
  17.1 92.8 %copy-start.113 = (f32[32]{0:T(128)}, f32[32]{0:T(128)S(1)}, u32[]{:S(2)}) copy-start(f32[32]{0:T(128)S(1)} %get-tuple-element.59) | copy-start | bytes 388
  20.7 49.3 %copy-start.65 = (bf16[768,3,192]{0,2,1:T(8,128)(2,1)}, bf16[768,3,192]{0,2,1:T(8,128)(2,1)S(1)}, u32[]{:S(2)}) copy-start(bf16[768,3,192]{0,2,1:T(8,128)(2,1)S(1)} %get-tuple-element.53) | copy-start | bytes 2654212
  75.6 7.0 copy-start.18
  93.4 71.4 %reduce-scatter.13.cloned.1.call-start = ((), (), s32[]{:S(2)}) async-start(), calls=%async_computation.14 | async-start | bytes 3932160 | tf_op jit(solution)/shard_map/reduce_scatter | solution.py:197
  118.0 5.9 copy-start.3
  118.0 70.6 %all-gather.21.cloned.1.call-start = ((), (), s32[]{:S(2)}) async-start(), calls=%async_computation.20 | async-start | bytes 2457600 | tf_op jit(solution)/shard_map/all_gather | solution.py:173
  127.6 91.5 %all-gather.17.cloned.1.call-start = ((), (), s32[]{:S(2)}) async-start(), calls=%async_computation.15 | async-start | bytes 3932160 | tf_op jit(solution)/shard_map/all_gather | solution.py:172
  166.7 21.9 %copy-start.69 = (bf16[768,3,192]{0,2,1:T(8,128)(2,1)S(1)}, bf16[768,3,192]{0,2,1:T(8,128)(2,1)}, u32[]{:S(2)}) copy-start(bf16[768,3,192]{0,2,1:T(8,128)(2,1)} %get-tuple-element.50) | copy-start | bytes 2654212
  168.1 84.7 %reduce-scatter.21.cloned.1.call-start = ((), (), s32[]{:S(2)}) async-start(), calls=%async_computation.21 | async-start | bytes 2457600 | tf_op jit(solution)/shard_map/reduce_scatter | solution.py:200
  198.0 7.5 copy-start.40
  218.0 75.8 %reduce-scatter.15.cloned.1.call-start = ((), (), s32[]{:S(2)}) async-start(), calls=%async_computation.16 | async-start | bytes 3932160 | tf_op jit(solution)/shard_map/reduce_scatter | solution.py:197
  247.9 69.8 %all-gather.23.cloned.1.call-start = ((), (), s32[]{:S(2)}) async-start(), calls=%async_computation.22 | async-start | bytes 2457600 | tf_op jit(solution)/shard_map/all_gather | solution.py:173
  256.0 85.0 %all-gather.31.cloned.1.call-start = ((), (), s32[]{:S(2)}) async-start(), calls=%async_computation.29 | async-start | bytes 2457600 | tf_op jit(solution)/shard_map/all_gather | solution.py:220
  256.6 115.1 %all-gather.19.cloned.1.call-start = ((), (), s32[]{:S(2)}) async-start(), calls=%async_computation.17 | async-start | bytes 3932160 | tf_op jit(solution)/shard_map/all_gather | solution.py:172
  297.0 104.6 %all-gather.25.cloned.1.call-start = ((), (), s32[]{:S(2)}) async-start(), calls=%async_computation.24 | async-start | bytes 3932160 | tf_op jit(solution)/shard_map/all_gather | solution.py:219
  297.6 137.0 %reduce-scatter.29.cloned.1.call-start = ((), (), s32[]{:S(2)}) async-start(), calls=%async_computation.30 | async-start | bytes 2457600 | tf_op jit(solution)/shard_map/reduce_scatter | solution.py:273
  341.0 8.3 copy-start.122
  352.3 122.6 %reduce-scatter.25.cloned.1.call-start = ((), (), s32[]{:S(2)}) async-start(), calls=%async_computation.25 | async-start | bytes 3932160 | tf_op jit(solution)/shard_map/reduce_scatter | solution.py:270
  401.7 10.1 copy-start.123
  415.9 82.9 %all-gather.33.cloned.1.call-start = ((), (), s32[]{:S(2)}) async-start(), calls=%async_computation.31 | async-start | bytes 2457600 | tf_op jit(solution)/shard_map/all_gather | solution.py:220
  439.9 103.8 %all-gather.27.cloned.1.call-start = ((), (), s32[]{:S(2)}) async-start(), calls=%async_computation.26 | async-start | bytes 3932160 | tf_op jit(solution)/shard_map/all_gather | solution.py:219
  479.6 107.6 %reduce-scatter.31.cloned.1.call-start = ((), (), s32[]{:S(2)}) async-start(), calls=%async_computation.32 | async-start | bytes 2457600 | tf_op jit(solution)/shard_map/reduce_scatter | solution.py:273
  537.0 63.3 %reduce-scatter.23.cloned.1.call-start = ((), (), s32[]{:S(2)}) async-start(), calls=%async_computation.23 | async-start | bytes 2457600 | tf_op jit(solution)/shard_map/reduce_scatter | solution.py:200
  543.3 97.4 %reduce-scatter.27.cloned.1.call-start = ((), (), s32[]{:S(2)}) async-start(), calls=%async_computation.27 | async-start | bytes 3932160 | tf_op jit(solution)/shard_map/reduce_scatter | solution.py:270
  578.0 103.1 %reduce-scatter.17.cloned.1.call-start = ((), (), s32[]{:S(2)}) async-start(), calls=%async_computation.18 | async-start | bytes 3932160 | tf_op jit(solution)/shard_map/reduce_scatter | solution.py:197
  587.1 117.9 %all-gather.35.cloned.1.call-start = ((), (), s32[]{:S(2)}) async-start(), calls=%async_computation.33 | async-start | bytes 2457600 | tf_op jit(solution)/shard_map/all_gather | solution.py:220
  604.2 131.5 %all-gather.29.cloned.1.call-start = ((), (), s32[]{:S(2)}) async-start(), calls=%async_computation.28 | async-start | bytes 3932160 | tf_op jit(solution)/shard_map/all_gather | solution.py:219
  685.2 154.6 %reduce-scatter.35.cloned.1.call-start = ((), (), s32[]{:S(2)}) async-start(), calls=%async_computation.35 | async-start | bytes 2457600 | tf_op jit(solution)/shard_map/reduce_scatter | solution.py:273
  698.2 6.8 copy-start.117
  705.0 7.0 copy-start.5
  705.0 7.0 copy-start.88
  723.0 12.7 %copy-start.116 = (bf16[32]{0:T(256)(128)(2,1)S(1)}, bf16[32]{0:T(256)(128)(2,1)}, u32[]{:S(2)}) copy-start(bf16[32]{0:T(256)(128)(2,1)} %get-tuple-element.57) | copy-start | bytes 196
  767.0 78.4 %reduce-scatter.33.cloned.1.call-start = ((), (), s32[]{:S(2)}) async-start(), calls=%async_computation.34 | async-start | bytes 3932160 | tf_op jit(solution)/shard_map/reduce_scatter | solution.py:270
  769.6 8.5 copy-start.33
  769.6 8.5 copy-start.38
  791.5 7.3 slice-start
  803.4 5.9 copy-start.89
  803.4 342.2 %all-reduce.5.cloned.1.call-start = ((), (), s32[]{:S(2)}) async-start(), calls=%async_computation.36 | async-start | bytes 18874368 | tf_op jit(solution)/shard_map/psum | solution.py:299
  803.6 5.7 copy-start.90
  803.6 5.7 copy-start.91
  (109 other events, 290.3 us)
Sparse Core Ops, SparseCore 0:
  14.7 24.5 all-gather.12
  41.4 28.4 all-gather.14
  93.5 30.3 reduce-scatter.18
  126.9 37.8 reduce-scatter.12
  166.8 21.8 all-gather.20
  190.6 28.4 all-gather.16
  222.3 30.3 reduce-scatter.20
  255.8 37.8 reduce-scatter.14
  295.9 21.8 all-gather.22
  319.2 21.8 all-gather.30
  343.2 28.4 all-gather.18
  373.1 28.4 all-gather.24
  404.2 30.3 reduce-scatter.28
  437.0 37.8 reduce-scatter.24
  476.9 21.8 all-gather.32
  500.8 28.4 all-gather.26
  537.1 30.3 reduce-scatter.30
  569.9 30.3 reduce-scatter.22
  602.8 37.8 reduce-scatter.26
  643.1 37.8 reduce-scatter.16
  683.2 21.8 all-gather.34
  707.2 28.4 all-gather.28
  767.1 30.3 reduce-scatter.34
  803.5 37.7 reduce-scatter.32
  846.3 299.1 all-reduce.4
where the time goes:
time: 1170 us; the launch traced here: 1160 us
  waiting for transfers between devices  633 us (54%)
  matrix products  245 us (21%)
  local copies, waits for them, and re-layouts  130 us (11%)
  other arithmetic  84.9 us (7%)
  blocking collectives  51.5 us (4%)
  between operations  16 us (1%)
    psum x1, waiting for transfers between devices, per_device(): lax.psum(grad.astype(jnp.bfloat16), 'dp').astype(jnp.float32)  242 us
    reduce_scatter x6, waiting for transfers between devices, per_device(): lax.psum_scatter(text_part.astype(jnp.bfloat16), 'mp', scatter_dimension=...  171 us
    dot_general x20, matrix products, linear(): jnp.einsum('pld,de->ple', activation, weight, preferred_element_type=jnp....  82 us
    dot_general x20, matrix products, linear_back(): jnp.einsum('ple,de->pld', gradient, weight, preferred_element_type=jnp.fl...  68.1 us
    all_gather x3, waiting for transfers between devices, per_device(): lax.all_gather(visual_norm, 'mp', axis=0, tiled=True)  58.5 us
    all_gather x3, waiting for transfers between devices, per_device(): lax.all_gather(text_norm, 'mp', axis=0, tiled=True)  47.1 us
    all_gather x3, waiting for transfers between devices, per_device(): lax.all_gather(visual_back.astype(jnp.bfloat16), 'mp', axis=0, tiled=True)  42.2 us
    psum x1, blocking collectives, per_device(): gain_grads, shift_grads = lax.psum((gain_grads, shift_grads), 'dp')  40.7 us
  transfers between devices with their start and end apart: 25, of which 21 were waited for; matrix products, arithmetic and copies ran while one was open for 31% of the time, Pallas kernels for 0%

commit v1 on v0

--- a/solution.py
+++ b/solution.py
@@ -1,3 +1,4 @@
+import functools
 import jax
 import jax.numpy as jnp
 from jax import lax
@@ -5,6 +6,33 @@
 
 HEAD = 64
 EPSILON = 1e-05
+
+
+def heads_handle(vec, join_dim):
+    f_next = lax.psum(1, "mp")
+    left_arr, carry_out, found_now = (f_next, lax.axis_index("mp"), vec.shape[join_dim])
+    kept_rows = tuple(((idx, (idx + 1) % left_arr) for idx in range(left_arr)))
+    samples = tuple(((idx, (idx - 1) % left_arr) for idx in range(left_arr)))
+    now = jnp.zeros(
+        (*vec.shape[:join_dim], left_arr * found_now, *vec.shape[join_dim + 1 :]), vec.dtype
+    )
+    now = lax.dynamic_update_slice_in_dim(now, vec, carry_out * found_now, axis=join_dim)
+    near = left_arr // 2
+    current_arr = heard = vec
+    for i0 in [*range(1, near + 1)]:
+        current_arr = lax.ppermute(current_arr, axis_name="mp", perm=kept_rows)
+        now = lax.dynamic_update_slice_in_dim(
+            now, current_arr, (carry_out - i0) % left_arr * found_now, axis=join_dim
+        )
+        if i0 < left_arr - near:
+            heard = lax.ppermute(heard, "mp", samples)
+            now = lax.dynamic_update_slice_in_dim(
+                now, heard, (carry_out + i0) % left_arr * found_now, axis=join_dim
+            )
+    return now
+
+
+reach_sources_all = functools.partial(heads_handle, join_dim=0)
 
 
 def normalize(values, gain, shift):
@@ -217,7 +245,7 @@
     for sublayer in (2, 1, 0):
         text_branch, visual_branch = (
             lax.all_gather(text_back.astype(jnp.bfloat16), "mp", axis=0, tiled=True),
-            lax.all_gather(visual_back.astype(jnp.bfloat16), "mp", axis=0, tiled=True),
+            reach_sources_all(visual_back.astype(jnp.bfloat16)),
         )
         text_rows, visual_rows = gathered[sublayer]
         text_saved, visual_saved = saved[sublayer]

time: 1170 us -> 1120 us (0.957)
  waiting for transfers between devices: 633 us -> 580 us
    ppermute x0 -> x9, waiting for transfers between devices: none -> 75.8 us  [the longest x6 69.9 us: heads_handle(): current_arr = lax.ppermute(current_arr, axis_name='mp', perm=kept_rows)]
    reduce_scatter x6, waiting for transfers between devices: 171 us -> 113 us  [per_device(): lax.psum_scatter(text_part.astype(jnp.bfloat16), 'mp', scatter_dimension=...]
    all_gather x3 -> x0, waiting for transfers between devices: 42.2 us -> none  [per_device(): lax.all_gather(visual_back.astype(jnp.bfloat16), 'mp', axis=0, tiled=True)]
    all_gather x3, waiting for transfers between devices: 47.1 us -> 24.3 us  [per_device(): lax.all_gather(text_norm, 'mp', axis=0, tiled=True)]
    reduce_scatter x6, waiting for transfers between devices: 39.3 us -> 61.9 us  [per_device(): lax.psum_scatter(visual_part.astype(jnp.bfloat16), 'mp', scatter_dimensio...]
    all_gather x3, waiting for transfers between devices: 58.5 us -> 38.4 us  [per_device(): lax.all_gather(visual_norm, 'mp', axis=0, tiled=True)]
    unnamed x264 -> x282, local copies, waits for them, and re-layouts: 27.2 us -> 29.8 us
  transfers between devices with their start and end apart: 25 -> 31, of which waited for: 21 -> 21; matrix products, arithmetic and copies ran while one was open for 31% -> 33% of each run, Pallas kernels for 0% -> 0%
where the time goes in v1:
time: 1120 us; the launch traced here: 1110 us
  waiting for transfers between devices  580 us (52%)
  matrix products  243 us (22%)
  local copies, waits for them, and re-layouts  132 us (12%)
  other arithmetic  81.3 us (7%)
  blocking collectives  51.8 us (5%)
  between operations  16.5 us (1%)
    psum x1, waiting for transfers between devices, per_device(): lax.psum(grad.astype(jnp.bfloat16), 'dp').astype(jnp.float32)  242 us
    reduce_scatter x6, waiting for transfers between devices, per_device(): lax.psum_scatter(text_part.astype(jnp.bfloat16), 'mp', scatter_dimension=...  113 us
    dot_general x20, matrix products, linear(): jnp.einsum('pld,de->ple', activation, weight, preferred_element_type=jnp....  78.7 us
    ppermute x6, waiting for transfers between devices, heads_handle(): current_arr = lax.ppermute(current_arr, axis_name='mp', perm=kept_rows)  69.9 us
    dot_general x20, matrix products, linear_back(): jnp.einsum('ple,de->pld', gradient, weight, preferred_element_type=jnp.fl...  66.4 us
    reduce_scatter x6, waiting for transfers between devices, per_device(): lax.psum_scatter(visual_part.astype(jnp.bfloat16), 'mp', scatter_dimensio...  61.9 us
    psum x1, blocking collectives, per_device(): gain_grads, shift_grads = lax.psum((gain_grads, shift_grads), 'dp')  41.2 us
    dot_general x20, matrix products, weight_grad(): jnp.einsum('pld,ple->de', activation, gradient, preferred_element_type=jn...  40.3 us
  transfers between devices with their start and end apart: 31, of which 21 were waited for; matrix products, arithmetic and copies ran while one was open for 33% of the time, Pallas kernels for 0%

profile of v1, /device:TPU:0, one launch (start us, length us, event | category | flops | bytes accessed | tf_op | source)
XLA Modules:
  0.0 1113.5 jit_solution(6706882108421482345)
XLA Ops:
  20.6 18.7 %all-gather.10.cloned.1.call-done = bf16[32,40,768]{2,1,0:T(8,128)(2,1)} async-done(((bf16[8,40,768]{2,1,0:T(8,128)(2,1)}), bf16[32,40,768]{2,1,0:T(8,128)(2,1)}) %all-gather.10.cloned.1.call-update) | async-done | bytes 1966096 | tf_op jit(solution)/shard_map/all_gather | solution.py:201
  46.3 23.6 %all-gather.12.cloned.1.call-done = bf16[32,64,768]{2,1,0:T(8,128)(2,1)} async-done(((bf16[8,64,768]{2,1,0:T(8,128)(2,1)}), bf16[32,64,768]{2,1,0:T(8,128)(2,1)}) %all-gather.12.cloned.1.call-update) | async-done | bytes 3145744 | tf_op jit(solution)/shard_map/all_gather | solution.py:200
  69.9 3.9 convolution_convert_fusion.18
  82.9 3.9 convolution_convert_fusion.3
  86.9 38.0 %reduce-scatter.13.cloned.1.call-done = bf16[8,64,768]{2,1,0:T(8,128)(2,1)} async-done(((bf16[32,64,768]{2,1,0:T(8,128)(2,1)}), bf16[8,64,768]{2,1,0:T(8,128)(2,1)}) %reduce-scatter.13.cloned.1.call-update) | async-done | bytes 786448 | tf_op jit(solution)/shard_map/reduce_scatter | solution.py:225
  132.1 3.9 convolution_convert_fusion.13
  137.9 4.4 convolution_convert_fusion.14
  165.9 4.2 convolution_convert_fusion.17
  178.2 3.9 convolution_convert_fusion.2
  182.2 8.1 reduce-scatter.19.cloned.1.call-done
  194.0 37.1 %reduce-scatter.15.cloned.1.call-done = bf16[8,64,768]{2,1,0:T(8,128)(2,1)} async-done(((bf16[32,64,768]{2,1,0:T(8,128)(2,1)}), bf16[8,64,768]{2,1,0:T(8,128)(2,1)}) %reduce-scatter.15.cloned.1.call-update) | async-done | bytes 786448 | tf_op jit(solution)/shard_map/reduce_scatter | solution.py:225
  235.4 19.8 %all-gather.18.cloned.1.call-done = bf16[32,40,768]{2,1,0:T(8,128)(2,1)} async-done(((bf16[8,40,768]{2,1,0:T(8,128)(2,1)}), bf16[32,40,768]{2,1,0:T(8,128)(2,1)}) %all-gather.18.cloned.1.call-update) | async-done | bytes 1966096 | tf_op jit(solution)/shard_map/all_gather | solution.py:201
  289.0 7.6 fusion.85
  296.6 19.3 %all-gather.22.cloned.1.call-done = bf16[32,64,768]{2,1,0:T(8,128)(2,1)} async-done(((bf16[8,64,768]{2,1,0:T(8,128)(2,1)}), bf16[32,64,768]{2,1,0:T(8,128)(2,1)}) %all-gather.22.cloned.1.call-update) | async-done | bytes 3145744 | tf_op jit(solution)/shard_map/all_gather | solution.py:247
  315.9 8.5 fusion.6
  326.1 4.0 convolution_convert_fusion
  330.1 18.6 %reduce-scatter.21.cloned.1.call-done = bf16[8,40,768]{2,1,0:T(8,128)(2,1)} async-done(((bf16[32,40,768]{2,1,0:T(8,128)(2,1)}), bf16[8,40,768]{2,1,0:T(8,128)(2,1)}) %reduce-scatter.21.cloned.1.call-update) | async-done | bytes 491536 | tf_op jit(solution)/shard_map/reduce_scatter | solution.py:228
  352.1 37.7 %reduce-scatter.25.cloned.1.call-done = bf16[8,64,768]{2,1,0:T(8,128)(2,1)} async-done(((bf16[32,64,768]{2,1,0:T(8,128)(2,1)}), bf16[8,64,768]{2,1,0:T(8,128)(2,1)}) %reduce-scatter.25.cloned.1.call-update) | async-done | bytes 786448 | tf_op jit(solution)/shard_map/reduce_scatter | solution.py:298
  396.3 17.5 %collective-permute-done = bf16[8,40,768]{2,1,0:T(8,128)(2,1)} collective-permute-done((bf16[8,40,768]{2,1,0:T(8,128)(2,1)}, bf16[8,40,768]{2,1,0:T(8,128)(2,1)}, u32[]{:S(2)}, u32[]{:S(2)}) %collective-permute-start) | collective-permute-done | bytes 491552 | tf_op jit(solution)/shard_map/ppermute | solution.py:23
  420.0 4.2 collective-permute-done.2
  429.8 7.8 fusion.13
  442.0 6.4 convolution_convert_fusion.5
  452.7 3.9 convolution_convert_fusion.12
  459.1 4.6 multiply_reduce_fusion
  470.8 4.4 fusion.36
  487.7 8.6 convolution_convert_fusion.1
  498.2 20.1 %reduce-scatter.23.cloned.1.call-done = bf16[8,40,768]{2,1,0:T(8,128)(2,1)} async-done(((bf16[32,40,768]{2,1,0:T(8,128)(2,1)}), bf16[8,40,768]{2,1,0:T(8,128)(2,1)}) %reduce-scatter.23.cloned.1.call-update) | async-done | bytes 491536 | tf_op jit(solution)/shard_map/reduce_scatter | solution.py:228
  523.7 11.1 collective-permute-done.3
  534.9 13.3 %collective-permute-done.5 = bf16[8,40,768]{2,1,0:T(8,128)(2,1)S(1)} collective-permute-done((bf16[8,40,768]{2,1,0:T(8,128)(2,1)S(1)}, bf16[8,40,768]{2,1,0:T(8,128)(2,1)S(1)}, u32[]{:S(2)}, u32[]{:S(2)}) %collective-permute-start.5) | collective-permute-done | bytes 491552 | tf_op jit(solution)/shard_map/ppermute | solution.py:23
  587.2 3.8 copy.219
  591.0 4.1 reshape.443
  598.7 5.8 fusion.46
  608.2 4.4 fusion.210
  612.7 5.2 fusion.44
  619.2 15.0 %reduce-scatter.31.cloned.1.call-done = bf16[8,40,768]{2,1,0:T(8,128)(2,1)} async-done(((bf16[32,40,768]{2,1,0:T(8,128)(2,1)}), bf16[8,40,768]{2,1,0:T(8,128)(2,1)}) %reduce-scatter.31.cloned.1.call-update) | async-done | bytes 491536 | tf_op jit(solution)/shard_map/reduce_scatter | solution.py:301
  643.9 11.7 %collective-permute-done.6 = bf16[8,40,768]{2,1,0:T(8,128)(2,1)S(1)} collective-permute-done((bf16[8,40,768]{2,1,0:T(8,128)(2,1)S(1)}, bf16[8,40,768]{2,1,0:T(8,128)(2,1)S(1)}, u32[]{:S(2)}, u32[]{:S(2)}) %collective-permute-start.6) | collective-permute-done | bytes 491552 | tf_op jit(solution)/shard_map/ppermute | solution.py:23
  657.1 5.9 collective-permute-done.7
  663.1 12.1 %collective-permute-done.8 = bf16[8,40,768]{2,1,0:T(8,128)(2,1)S(1)} collective-permute-done((bf16[8,40,768]{2,1,0:T(8,128)(2,1)S(1)}, bf16[8,40,768]{2,1,0:T(8,128)(2,1)S(1)}, u32[]{:S(2)}, u32[]{:S(2)}) %collective-permute-start.8) | collective-permute-done | bytes 491552 | tf_op jit(solution)/shard_map/ppermute | solution.py:23
  689.5 3.8 fusion.171
  693.3 3.9 fusion.49
  718.8 8.5 fusion.45
  731.9 3.8 convolution_convert_fusion.8
  735.7 5.1 fusion.172
  748.5 4.1 add_convert_fusion
  753.1 5.7 fusion.43
  797.6 10.7 all-reduce.2
  808.3 41.2 %all-reduce = (f32[6,768]{1,0:T(8,128)}, f32[6,768]{1,0:T(8,128)}) all-reduce(bf16[6,768]{1,0:T(8,128)(2,1)S(1)} %get-tuple-element.40, bf16[6,768]{1,0:T(8,128)(2,1)S(1)} %get-tuple-element.41), channel_id=1, replica_groups=mesh['dp'=8,'mp'=4] {'dp'}, use_global_device_ids=true, to_apply=%region_59.60 | all-reduce | flops 9216 | bytes 55296 | tf_op jit(solution)/shard_map/psum | solution.py:330
  852.4 242.3 %all-reduce.5.cloned.1.call-done = (bf16[4,768,3,192]{1,3,2,0:T(8,128)(2,1)}, bf16[4,192,768]{2,1,0:T(8,128)(2,1)}, bf16[2,768,768]{2,1,0:T(8,128)(2,1)}, bf16[2,768,768]{2,1,0:T(8,128)(2,1)}) async-done(((bf16[4,768,3,192]{1,3,2,0:T(8,128)(2,1)}, bf16[4,192,768]{2,1,0:T(8,128)(2,1)}, bf16[2,768,768]{2,1,0:T(8,128)(2,1)}, bf16[2,768,768]{2,1,0:T(8,128)(2,1)}), (bf16[4,768,3,192]{1,3,2,0:T(8,128)(2,1)}, ...) | async-done | bytes 9437200 | tf_op jit(solution)/shard_map/psum | solution.py:327
  (562 shorter events, 332.7 us)
Async XLA Ops:
  7.2 7.4 copy-start
  7.2 32.1 %all-gather.10.cloned.1.call-start = ((), (), s32[]{:S(2)}) async-start(), calls=%async_computation.12 | async-start | bytes 2457600 | tf_op jit(solution)/shard_map/all_gather | solution.py:201
  14.5 55.4 %all-gather.12.cloned.1.call-start = ((), (), s32[]{:S(2)}) async-start(), calls=%async_computation.13 | async-start | bytes 3932160 | tf_op jit(solution)/shard_map/all_gather | solution.py:200
  16.5 108.4 %reduce-scatter.13.cloned.1.call-start = ((), (), s32[]{:S(2)}) async-start(), calls=%async_computation.14 | async-start | bytes 3932160 | tf_op jit(solution)/shard_map/reduce_scatter | solution.py:225
  17.1 61.8 %copy-start.122 = (f32[32]{0:T(128)}, f32[32]{0:T(128)S(1)}, u32[]{:S(2)}) copy-start(f32[32]{0:T(128)S(1)} %get-tuple-element.64) | copy-start | bytes 388
  17.1 131.2 %copy-start.120 = (f32[32]{0:T(128)}, f32[32]{0:T(128)S(1)}, u32[]{:S(2)}) copy-start(f32[32]{0:T(128)S(1)} %get-tuple-element.63) | copy-start | bytes 388
  20.6 49.3 %copy-start.73 = (bf16[768,3,192]{0,2,1:T(8,128)(2,1)}, bf16[768,3,192]{0,2,1:T(8,128)(2,1)S(1)}, u32[]{:S(2)}) copy-start(bf16[768,3,192]{0,2,1:T(8,128)(2,1)S(1)} %get-tuple-element.55) | copy-start | bytes 2654212
  86.9 70.0 %all-gather.14.cloned.1.call-start = ((), (), s32[]{:S(2)}) async-start(), calls=%async_computation.15 | async-start | bytes 3932160 | tf_op jit(solution)/shard_map/all_gather | solution.py:200
  128.2 62.1 %reduce-scatter.19.cloned.1.call-start = ((), (), s32[]{:S(2)}) async-start(), calls=%async_computation.19 | async-start | bytes 2457600 | tf_op jit(solution)/shard_map/reduce_scatter | solution.py:228
  137.9 7.0 copy-start.22
  155.6 75.5 %reduce-scatter.15.cloned.1.call-start = ((), (), s32[]{:S(2)}) async-start(), calls=%async_computation.16 | async-start | bytes 3932160 | tf_op jit(solution)/shard_map/reduce_scatter | solution.py:225
  182.1 8.2 copy-start.3
  182.1 73.0 %all-gather.18.cloned.1.call-start = ((), (), s32[]{:S(2)}) async-start(), calls=%async_computation.20 | async-start | bytes 2457600 | tf_op jit(solution)/shard_map/all_gather | solution.py:201
  194.0 95.0 %all-gather.16.cloned.1.call-start = ((), (), s32[]{:S(2)}) async-start(), calls=%async_computation.17 | async-start | bytes 3932160 | tf_op jit(solution)/shard_map/all_gather | solution.py:200
  234.4 81.5 %all-gather.22.cloned.1.call-start = ((), (), s32[]{:S(2)}) async-start(), calls=%async_computation.24 | async-start | bytes 3932160 | tf_op jit(solution)/shard_map/all_gather | solution.py:247
  235.2 113.6 %reduce-scatter.21.cloned.1.call-start = ((), (), s32[]{:S(2)}) async-start(), calls=%async_computation.21 | async-start | bytes 2457600 | tf_op jit(solution)/shard_map/reduce_scatter | solution.py:228
  288.7 101.1 %reduce-scatter.25.cloned.1.call-start = ((), (), s32[]{:S(2)}) async-start(), calls=%async_computation.25 | async-start | bytes 3932160 | tf_op jit(solution)/shard_map/reduce_scatter | solution.py:298
  315.9 10.1 copy-start.131
  330.1 95.9 %all-gather.20.cloned.1.call-start = ((), (), s32[]{:S(2)}) async-start(), calls=%async_computation.22 | async-start | bytes 2457600 | tf_op jit(solution)/shard_map/all_gather | solution.py:201
  352.0 100.6 %all-gather.24.cloned.1.call-start = ((), (), s32[]{:S(2)}) async-start(), calls=%async_computation.26 | async-start | bytes 3932160 | tf_op jit(solution)/shard_map/all_gather | solution.py:247
  394.5 102.0 %reduce-scatter.29.cloned.1.call-start = ((), (), s32[]{:S(2)}) async-start(), calls=%async_computation.29 | async-start | bytes 2457600 | tf_op jit(solution)/shard_map/reduce_scatter | solution.py:301
  394.5 19.3 %collective-permute-start = (bf16[8,40,768]{2,1,0:T(8,128)(2,1)}, bf16[8,40,768]{2,1,0:T(8,128)(2,1)}, u32[]{:S(2)}, u32[]{:S(2)}) collective-permute-start(bf16[8,40,768]{2,1,0:T(8,128)(2,1)} %param.21), channel_id=1, source_target_pairs={{0,1},{1,2},{2,3},{3,0},{4,5},{5,6},{6,7},{7,4},{8,9},{9,10},{10,1... | collective-permute-start | bytes 1474568 | tf_op jit(solution)/shard_map/ppermute | solution.py:23
  394.6 23.6 %collective-permute-start.1 = (bf16[8,40,768]{2,1,0:T(8,128)(2,1)}, bf16[8,40,768]{2,1,0:T(8,128)(2,1)}, u32[]{:S(2)}, u32[]{:S(2)}) collective-permute-start(bf16[8,40,768]{2,1,0:T(8,128)(2,1)} %param.21), channel_id=1, source_target_pairs={{0,3},{1,0},{2,1},{3,2},{4,7},{5,4},{6,5},{7,6},{8,11},{9,8},{10,9... | collective-permute-start | bytes 1474568 | tf_op jit(solution)/shard_map/ppermute | solution.py:28
  413.8 10.4 collective-permute-start.2
  429.8 7.9 copy-start.137
  429.8 9.1 copy-start.132
  442.0 76.4 %reduce-scatter.23.cloned.1.call-start = ((), (), s32[]{:S(2)}) async-start(), calls=%async_computation.23 | async-start | bytes 2457600 | tf_op jit(solution)/shard_map/reduce_scatter | solution.py:228
  448.4 156.1 %reduce-scatter.27.cloned.1.call-start = ((), (), s32[]{:S(2)}) async-start(), calls=%async_computation.27 | async-start | bytes 3932160 | tf_op jit(solution)/shard_map/reduce_scatter | solution.py:298
  487.5 120.7 %reduce-scatter.17.cloned.1.call-start = ((), (), s32[]{:S(2)}) async-start(), calls=%async_computation.18 | async-start | bytes 3932160 | tf_op jit(solution)/shard_map/reduce_scatter | solution.py:225
  496.4 137.8 %reduce-scatter.31.cloned.1.call-start = ((), (), s32[]{:S(2)}) async-start(), calls=%async_computation.30 | async-start | bytes 2457600 | tf_op jit(solution)/shard_map/reduce_scatter | solution.py:301
  521.9 12.9 %collective-permute-start.3 = (bf16[8,40,768]{2,1,0:T(8,128)(2,1)S(1)}, bf16[8,40,768]{2,1,0:T(8,128)(2,1)S(1)}, u32[]{:S(2)}, u32[]{:S(2)}) collective-permute-start(bf16[8,40,768]{2,1,0:T(8,128)(2,1)S(1)} %get-tuple-element.46), channel_id=1, source_target_pairs={{0,1},{1,2},{2,3},{3,0},{4,5},{5,6},{6,7},{7,4},{8,9},{9,10},{10,1... | collective-permute-start | bytes 1474568 | tf_op jit(solution)/shard_map/ppermute | solution.py:23
  522.0 12.9 %collective-permute-start.4 = (bf16[8,40,768]{2,1,0:T(8,128)(2,1)S(1)}, bf16[8,40,768]{2,1,0:T(8,128)(2,1)S(1)}, u32[]{:S(2)}, u32[]{:S(2)}) collective-permute-start(bf16[8,40,768]{2,1,0:T(8,128)(2,1)S(1)} %get-tuple-element.46), channel_id=1, source_target_pairs={{0,3},{1,0},{2,1},{3,2},{4,7},{5,4},{6,5},{7,6},{8,11},{9,8},{10,9... | collective-permute-start | bytes 1474568 | tf_op jit(solution)/shard_map/ppermute | solution.py:28
  534.8 13.5 %collective-permute-start.5 = (bf16[8,40,768]{2,1,0:T(8,128)(2,1)S(1)}, bf16[8,40,768]{2,1,0:T(8,128)(2,1)S(1)}, u32[]{:S(2)}, u32[]{:S(2)}) collective-permute-start(bf16[8,40,768]{2,1,0:T(8,128)(2,1)S(1)} %collective-permute-done.3), channel_id=1, source_target_pairs={{0,1},{1,2},{2,3},{3,0},{4,5},{5,6},{6,7},{7,4},{8,9},{9,10},{10,1... | collective-permute-start | bytes 1474568 | tf_op jit(solution)/shard_map/ppermute | solution.py:23
  586.8 106.5 %all-gather.26.cloned.1.call-start = ((), (), s32[]{:S(2)}) async-start(), calls=%async_computation.28 | async-start | bytes 3932160 | tf_op jit(solution)/shard_map/all_gather | solution.py:247
  612.7 175.2 %reduce-scatter.35.cloned.1.call-start = ((), (), s32[]{:S(2)}) async-start(), calls=%async_computation.32 | async-start | bytes 2457600 | tf_op jit(solution)/shard_map/reduce_scatter | solution.py:301
  639.5 16.1 %collective-permute-start.6 = (bf16[8,40,768]{2,1,0:T(8,128)(2,1)S(1)}, bf16[8,40,768]{2,1,0:T(8,128)(2,1)S(1)}, u32[]{:S(2)}, u32[]{:S(2)}) collective-permute-start(bf16[8,40,768]{2,1,0:T(8,128)(2,1)S(1)} %get-tuple-element.43), channel_id=1, source_target_pairs={{0,1},{1,2},{2,3},{3,0},{4,5},{5,6},{6,7},{7,4},{8,9},{9,10},{10,1... | collective-permute-start | bytes 1474568 | tf_op jit(solution)/shard_map/ppermute | solution.py:23
  641.0 14.8 %copy-start.85 = (bf16[32,40,192]{2,1,0:T(8,128)(2,1)S(1)}, bf16[32,40,192]{2,1,0:T(8,128)(2,1)}, u32[]{:S(2)}) copy-start(bf16[32,40,192]{2,1,0:T(8,128)(2,1)} %convert_element_type.546) | copy-start | bytes 1474564
  641.0 22.0 %collective-permute-start.7 = (bf16[8,40,768]{2,1,0:T(8,128)(2,1)S(1)}, bf16[8,40,768]{2,1,0:T(8,128)(2,1)S(1)}, u32[]{:S(2)}, u32[]{:S(2)}) collective-permute-start(bf16[8,40,768]{2,1,0:T(8,128)(2,1)S(1)} %get-tuple-element.43), channel_id=1, source_target_pairs={{0,3},{1,0},{2,1},{3,2},{4,7},{5,4},{6,5},{7,6},{8,11},{9,8},{10,9... | collective-permute-start | bytes 1474568 | tf_op jit(solution)/shard_map/ppermute | solution.py:28
  655.6 19.6 %collective-permute-start.8 = (bf16[8,40,768]{2,1,0:T(8,128)(2,1)S(1)}, bf16[8,40,768]{2,1,0:T(8,128)(2,1)S(1)}, u32[]{:S(2)}, u32[]{:S(2)}) collective-permute-start(bf16[8,40,768]{2,1,0:T(8,128)(2,1)S(1)} %collective-permute-done.6), channel_id=1, source_target_pairs={{0,1},{1,2},{2,3},{3,0},{4,5},{5,6},{6,7},{7,4},{8,9},{9,10},{10,1... | collective-permute-start | bytes 1474568 | tf_op jit(solution)/shard_map/ppermute | solution.py:23
  657.1 19.4 %copy-start.126 = (bf16[32]{0:T(256)(128)(2,1)S(1)}, bf16[32]{0:T(256)(128)(2,1)}, u32[]{:S(2)}) copy-start(bf16[32]{0:T(256)(128)(2,1)} %get-tuple-element.61) | copy-start | bytes 196
  676.5 6.2 copy-start.7
  676.5 6.2 copy-start.94
  716.7 76.8 %reduce-scatter.33.cloned.1.call-start = ((), (), s32[]{:S(2)}) async-start(), calls=%async_computation.31 | async-start | bytes 3932160 | tf_op jit(solution)/shard_map/reduce_scatter | solution.py:298
  718.8 8.5 copy-start.33
  718.8 8.5 copy-start.39
  740.8 7.3 slice-start
  752.7 6.1 copy-start.95
  752.7 342.0 %all-reduce.5.cloned.1.call-start = ((), (), s32[]{:S(2)}) async-start(), calls=%async_computation.33 | async-start | bytes 18874368 | tf_op jit(solution)/shard_map/psum | solution.py:327
  (124 other events, 334.2 us)
Sparse Core Ops, SparseCore 0:
  14.7 24.5 all-gather.9
  41.4 28.4 all-gather.11
  87.0 37.8 reduce-scatter.12
  128.3 28.5 all-gather.13
  159.8 30.3 reduce-scatter.18
  193.2 37.8 reduce-scatter.14
  233.3 21.8 all-gather.17
  257.3 28.4 all-gather.15
  287.4 28.4 all-gather.21
  318.3 30.3 reduce-scatter.20
  351.9 37.8 reduce-scatter.24
  391.8 29.3 all-gather.19
  423.3 29.3 all-gather.23
  455.1 30.3 reduce-scatter.28
  487.9 30.3 reduce-scatter.22
  520.7 40.5 reduce-scatter.26
  563.7 37.6 reduce-scatter.16
  603.8 30.3 reduce-scatter.30
  636.4 40.1 all-gather.25
  716.8 30.3 reduce-scatter.34
  752.8 37.5 reduce-scatter.32
  795.4 299.2 all-reduce.4
